TPU v7x, 32 devices: a whole 2x2x4 slice. The times are simulated.
32 devices in a mesh: row: 8 (over y, x, core), col: 4 (over z).
Axes of the slice: x: 2, y: 2, z: 4, core: 2. Of those that a mesh axis runs over, the one named last changes fastest.
Arguments:
- inputs: bfloat16 [32768, 261], P('row'), may hold values from -6 to 6
- latent: bfloat16 [512, 1024], P('row', 'col'), may hold values from -6 to 6
- gain_latent: float32 [1024], P('col'), may hold values from 0.25 to 1.75
- gain_inputs: float32 [261], replicated, may hold values from 0.25 to 1.75
- cross_query: bfloat16 [1024, 1024], P('col', 'row'), may hold values from -0.1875 to 0.1875
- cross_keys: bfloat16 [261, 1024], P(None, 'col'), may hold values from -0.375 to 0.375
- cross_values: bfloat16 [261, 1024], P(None, 'col'), may hold values from -0.375 to 0.375
- cross_output: bfloat16 [1024, 1024], P('col', 'row'), may hold values from -3 to 3
- cross_gain: float32 [1024], P('col'), may hold values from 0.25 to 1.75
- cross_up: bfloat16 [1024, 1024], P('row', 'col'), may hold values from -0.1875 to 0.1875
- cross_down: bfloat16 [1024, 1024], P('col', 'row'), may hold values from -0.1875 to 0.1875
- self_gain: float32 [1024], P('col'), may hold values from 0.25 to 1.75
- self_query: bfloat16 [1024, 1024], P('row', 'col'), may hold values from -0.1875 to 0.1875
- self_keys: bfloat16 [1024, 1024], P('row', 'col'), may hold values from -0.1875 to 0.1875
- self_values: bfloat16 [1024, 1024], P('row', 'col'), may hold values from -0.1875 to 0.1875
- self_output: bfloat16 [1024, 1024], P('col', 'row'), may hold values from -2 to 2
- self_mlp_gain: float32 [1024], P('col'), may hold values from 0.25 to 1.75
- self_mlp_up: bfloat16 [1024, 1024], P('row', 'col'), may hold values from -0.1875 to 0.1875
- self_mlp_down: bfloat16 [1024, 1024], P('col', 'row'), may hold values from -0.1875 to 0.1875
- cotangent: bfloat16 [16384, 1024], P('row', 'col'), may hold values from -6 to 6
Outputs:
- result: bfloat16 [16384, 1024], P('row', 'col')
- grad_inputs: float32 [32768, 261], P(('row', 'col'))
- grad_latent: float32 [512, 1024], P('row', 'col')
- grad_gain_latent: float32 [1024], P('col')
- grad_gain_inputs: float32 [261], replicated
- grad_cross_query: float32 [1024, 1024], P('col', 'row')
- grad_cross_keys: float32 [261, 1024], P(None, 'col')
- grad_cross_values: float32 [261, 1024], P(None, 'col')
- grad_cross_output: float32 [1024, 1024], P('col', 'row')
- grad_cross_gain: float32 [1024], P('col')
- grad_cross_up: float32 [1024, 1024], P('row', 'col')
- grad_cross_down: float32 [1024, 1024], P('col', 'row')
- grad_self_gain: float32 [1024], P('col')
- grad_self_query: float32 [1024, 1024], P('row', 'col')
- grad_self_keys: float32 [1024, 1024], P('row', 'col')
- grad_self_values: float32 [1024, 1024], P('row', 'col')
- grad_self_output: float32 [1024, 1024], P('col', 'row')
- grad_self_mlp_gain: float32 [1024], P('col')
- grad_self_mlp_up: float32 [1024, 1024], P('row', 'col')
- grad_self_mlp_down: float32 [1024, 1024], P('col', 'row')
All inputs are finite; a program needn't handle non-finite values.
Results may differ from a plain program's by a relative error of at most 0.039.
Values may be sent and summed in bfloat16 or wider, within the bound.
No kernel may reach another device: no remote copies, remote signals or barrier semaphores. Data moves between devices by JAX's collectives and lax.ppermute only.
A program may use at most 192 MiB of HBM per device.

v0:
```python
import jax
import jax.numpy as jnp
from jax import lax
from jax.sharding import PartitionSpec as P

HEADS = 8
M = 1024
EPSILON = 1e-05
BF = jnp.bfloat16
F32 = jnp.float32
BOTH = ("row", "col")


def nn(left, right):
    return lax.dot_general(left, right, (((1,), (0,)), ((), ())), preferred_element_type=F32)


def nt(left, right):
    return lax.dot_general(left, right, (((1,), (1,)), ((), ())), preferred_element_type=F32)


def tn(left, right):
    return lax.dot_general(left, right, (((0,), (0,)), ((), ())), preferred_element_type=F32)


def norm(values, gain):
    average = jnp.mean(values, axis=-1, keepdims=True)
    centred = values - average
    scale = lax.rsqrt(jnp.mean(centred * centred, axis=-1, keepdims=True) + EPSILON)
    hat = centred * scale
    return ((hat * gain).astype(BF), hat, scale)


def norm_back(upstream, gain, hat, scale):
    scaled = upstream * gain
    first = jnp.mean(scaled, axis=-1, keepdims=True)
    second = jnp.mean(scaled * hat, axis=-1, keepdims=True)
    return (scale * (scaled - first - hat * second), jnp.sum(upstream * hat, axis=0))


def gelu(values):
    return jax.nn.gelu(values, approximate=True)


def gelu_back(values, upstream):
    return jax.vjp(gelu, values)[1](upstream)[0].astype(BF)


def softmax(scores):
    exponent = jnp.exp(scores - jnp.max(scores, axis=-1, keepdims=True))
    return exponent / jnp.sum(exponent, axis=-1, keepdims=True)


def softmax_back(soft, upstream):
    return (soft * (upstream - jnp.sum(upstream * soft, axis=-1, keepdims=True))).astype(BF)


def local(
    inputs,
    latent,
    gain_latent,
    gain_inputs,
    cross_query,
    cross_keys,
    cross_values,
    cross_output,
    cross_gain,
    cross_up,
    cross_down,
    self_gain,
    self_query,
    self_keys,
    self_values,
    self_output,
    self_mlp_gain,
    self_mlp_up,
    self_mlp_down,
    cotangent,
):
    cols = lax.axis_size("col")
    rows = lax.axis_size("row")
    place = lax.axis_index("col")
    wide = latent.shape[1] * cols
    block = latent.shape[1]
    lat_count = latent.shape[0] * rows
    head_size = wide // HEADS
    in_width = inputs.shape[1]
    images = inputs.shape[0] // M
    share = max(1, cols // images)
    assert images * share == cols
    here = lat_count // share
    groups = [[image * share + part for part in range(share)] for image in range(images)]
    cross_scale = wide ** (-0.5)
    self_scale = head_size ** (-0.5)
    by_row = (cross_up, self_query, self_keys, self_values, self_mlp_up)
    by_col = (cross_query, cross_output, cross_down, self_output, self_mlp_down)
    stack = jnp.stack([item.T for item in by_col] + list(by_row))
    count = stack.shape[0]
    deep = stack.shape[1]
    whole = lax.all_gather(stack, BOTH, axis=0, tiled=False)
    whole = whole.reshape(rows, cols, count, deep, block)
    whole = whole.transpose(2, 0, 3, 1, 4).reshape(count, wide, wide)
    t_query, t_output, t_down, t_self_output, t_self_down, up, s_query, s_keys, s_values, s_up = [
        whole[index] for index in range(count)
    ]
    lat_all = lax.all_gather(latent, BOTH, axis=0, tiled=False)
    lat_all = lat_all.reshape(rows, cols, -1, block).transpose(0, 2, 1, 3).reshape(lat_count, wide)
    pair = lax.all_gather(jnp.concatenate([cross_keys, cross_values]), "col", axis=1, tiled=True)
    c_keys, c_values = (pair[:in_width], pair[in_width:])
    gains = lax.all_gather(
        jnp.stack([gain_latent, cross_gain, self_gain, self_mlp_gain]), "col", axis=1, tiled=True
    )
    g_lat, g_cross, g_self, g_mlp = [gains[index] for index in range(4)]
    grad_out_low = lax.all_to_all(cotangent, "col", split_axis=0, concat_axis=1, tiled=True)
    start = place % share * here
    lat = lax.dynamic_slice_in_dim(lat_all, start, here, axis=0).astype(F32)
    pixels = lax.dynamic_slice_in_dim(inputs, place // share * M, M, axis=0).astype(F32)
    lat_low, lat_hat, lat_scale = norm(lat, g_lat)
    queries = nt(lat_low, t_query).astype(BF)
    pix_low, pix_hat, pix_scale = norm(pixels, gain_inputs)
    key_rows = nn(pix_low, c_keys).astype(BF)
    values = nn(pix_low, c_values).astype(BF)
    soft = softmax(nt(queries, key_rows) * cross_scale)
    soft_low = soft.astype(BF)
    attended = nn(soft_low, values).astype(BF)
    state_one = lat + nt(attended, t_output)
    mlp_low, mlp_hat, mlp_scale = norm(state_one, g_cross)
    hidden = nn(mlp_low, up)
    active = gelu(hidden).astype(BF)
    state_two = state_one + nt(active, t_down)
    attn_low, attn_hat, attn_scale = norm(state_two, g_self)
    head_q = nn(attn_low, s_query).astype(BF)
    head_k = nn(attn_low, s_keys).astype(BF)
    head_v = nn(attn_low, s_values).astype(BF)
    if share > 1:
        head_k, head_v = [
            lax.all_gather(item, "col", axis_index_groups=groups, axis=0, tiled=True)
            for item in (head_k, head_v)
        ]

    def split(item):
        return item.reshape(item.shape[0], HEADS, head_size)

    def join(item):
        return item.astype(BF).reshape(item.shape[0], wide)

    def contract(form, left, right):
        return jnp.einsum(form, left, right, preferred_element_type=F32)

    hq, hk, hv = (split(head_q), split(head_k), split(head_v))
    self_soft = softmax(contract("qhd,khd->hqk", hq, hk) * self_scale)
    self_soft_low = self_soft.astype(BF)
    self_att = join(contract("hqk,khd->qhd", self_soft_low, hv))
    state_three = state_two + nt(self_att, t_self_output)
    last_low, last_hat, last_scale = norm(state_three, g_mlp)
    hidden_two = nn(last_low, s_up)
    active_two = gelu(hidden_two).astype(BF)
    result = (state_three + nt(active_two, t_self_down)).astype(BF)
    result = lax.all_to_all(result, "col", split_axis=1, concat_axis=0, tiled=True)
    grad_self_down = tn(grad_out_low, active_two)
    dh2 = gelu_back(hidden_two, nn(grad_out_low, t_self_down))
    grad_self_up = tn(last_low, dh2)
    back, gain_mlp = norm_back(nt(dh2, s_up), g_mlp, last_hat, last_scale)
    g3 = grad_out_low.astype(F32) + back
    g3_low = g3.astype(BF)
    grad_self_output = tn(g3_low, self_att)
    d_att = split(nn(g3_low, t_self_output).astype(BF))
    d_self = softmax_back(self_soft, contract("qhd,khd->hqk", d_att, hv))
    dq = join(contract("hqk,khd->qhd", d_self, hk) * self_scale)
    dk = contract("hqk,qhd->khd", d_self, hq) * self_scale
    dvv = contract("hqk,qhd->khd", self_soft_low, d_att)
    dk, dvv = (join(dk), join(dvv))
    if share > 1:
        dk, dvv = [
            lax.psum_scatter(item, "col", axis_index_groups=groups, scatter_dimension=0, tiled=True)
            for item in (dk, dvv)
        ]
    grad_query, grad_keys, grad_values = (tn(attn_low, dq), tn(attn_low, dk), tn(attn_low, dvv))
    dy = nt(dq, s_query) + nt(dk, s_keys) + nt(dvv, s_values)
    back, gain_self = norm_back(dy, g_self, attn_hat, attn_scale)
    g2 = g3 + back
    g2_low = g2.astype(BF)
    grad_down = tn(g2_low, active)
    dh1 = gelu_back(hidden, nn(g2_low, t_down))
    grad_up = tn(mlp_low, dh1)
    back, gain_cross = norm_back(nt(dh1, up), g_cross, mlp_hat, mlp_scale)
    g1 = g2 + back
    g1_low = g1.astype(BF)
    grad_output = tn(g1_low, attended)
    d_attended = nn(g1_low, t_output).astype(BF)
    d_scores = softmax_back(soft, nt(d_attended, values))
    d_queries = (nn(d_scores, key_rows) * cross_scale).astype(BF)
    d_keys = (tn(d_scores, queries) * cross_scale).astype(BF)
    d_values = tn(soft_low, d_attended).astype(BF)
    grad_cross_query = tn(d_queries, lat_low)
    grad_pair = jnp.concatenate([tn(pix_low, d_keys), tn(pix_low, d_values)])
    d_pix = nt(d_keys, c_keys) + nt(d_values, c_values)
    grad_inputs, gain_pix = norm_back(d_pix, gain_inputs, pix_hat, pix_scale)
    if share > 1:
        grad_inputs = lax.psum_scatter(
            grad_inputs, "col", axis_index_groups=groups, scatter_dimension=0, tiled=True
        )
    back, gain_lat = norm_back(nn(d_queries, t_query), g_lat, lat_hat, lat_scale)
    grad_lat = g1 + back
    if share > 1:
        grad_lat = lax.dynamic_update_slice_in_dim(
            jnp.zeros((lat_count, wide), F32), grad_lat, start, axis=0
        )

    def reduce(item):
        item = lax.psum_scatter(item, "row", scatter_dimension=0, tiled=False)
        return lax.psum_scatter(item, "col", scatter_dimension=0, tiled=False).astype(F32)

    grads = jnp.stack(
        [
            item.astype(BF)
            for item in (
                grad_cross_query,
                grad_output,
                grad_down,
                grad_self_output,
                grad_self_down,
                grad_up,
                grad_query,
                grad_keys,
                grad_values,
                grad_self_up,
            )
        ]
    )
    grads = grads.reshape(count, rows, deep, cols, block).transpose(1, 3, 0, 2, 4)
    grads = reduce(grads)
    grad_lat = reduce(grad_lat.astype(BF).reshape(rows, -1, cols, block).transpose(0, 2, 1, 3))
    grad_pair = lax.psum_scatter(
        grad_pair.astype(BF).reshape(-1, cols, block).transpose(1, 0, 2),
        "col",
        scatter_dimension=0,
        tiled=False,
    )
    grad_pair = lax.psum(grad_pair, "row").astype(F32)
    gain_all, gain_pix = lax.psum(
        (jnp.stack([gain_lat, gain_cross, gain_self, gain_mlp]), gain_pix), BOTH
    )
    gain_all = lax.dynamic_slice_in_dim(gain_all, place * block, block, axis=1)
    return (
        result,
        grad_inputs,
        grad_lat,
        gain_all[0],
        gain_pix,
        grads[0].T,
        grad_pair[:in_width],
        grad_pair[in_width:],
        grads[1].T,
        gain_all[1],
        grads[5],
        grads[2].T,
        gain_all[2],
        grads[6],
        grads[7],
        grads[8],
        grads[3].T,
        gain_all[3],
        grads[9],
        grads[4].T,
    )


def solution(mesh):
    rc, cr, c, cc = (P("row", "col"), P("col", "row"), P("col"), P(None, "col"))
    return jax.shard_map(
        local,
        mesh=mesh,
        in_specs=(
            P("row", None),
            rc,
            c,
            P(),
            cr,
            cc,
            cc,
            cr,
            c,
            rc,
            cr,
            c,
            rc,
            rc,
            rc,
            cr,
            c,
            rc,
            cr,
            rc,
        ),
        out_specs=(
            rc,
            P(BOTH, None),
            rc,
            c,
            P(),
            cr,
            cc,
            cc,
            cr,
            c,
            rc,
            cr,
            c,
            rc,
            rc,
            rc,
            cr,
            c,
            rc,
            cr,
        ),
        check_vma=False,
    )
```

profile of v0, /device:TPU:0, one launch (start us, length us, event | category | flops | bytes accessed | tf_op | source)
XLA Modules:
  0.0 815.1 jit_solution(8326261063209987246)
XLA Ops:
  15.9 6.4 all-to-all-start.1
  22.3 46.8 %all_gather.20 = f32[4,1024]{1,0:T(4,128)S(1)} all-gather(f32[4,256]{1,0:T(4,128)S(1)} %pad_maximum_fusion.2), channel_id=1, replica_groups=mesh['row'=8,'col'=4] {'col'}, dimensions={1}, use_global_device_ids=true | all-gather | bytes 20480 | tf_op jit(solution)/shard_map/all_gather | solution.py:110
  69.7 4.1 convolution_convert_fusion.10
  73.9 4.5 fusion.166
  78.3 41.6 %all-gather.8.cloned.1.call-done = bf16[2048,256]{1,0:T(8,128)(2,1)} async-done(((bf16[64,256]{1,0:T(8,128)(2,1)}), bf16[2048,256]{1,0:T(8,128)(2,1)}) %all-gather.8.cloned.1.call-update) | async-done | bytes 1048592 | tf_op jit(solution)/shard_map/all_gather | solution.py:106
  126.0 7.4 multiply_reduce_fusion.14
  135.5 120.6 %all-gather.10.cloned.1.call-done = bf16[320,128,256]{2,1,0:T(8,128)(2,1)} async-done(((bf16[10,128,256]{2,1,0:T(8,128)(2,1)}), bf16[320,128,256]{2,1,0:T(8,128)(2,1)}) %all-gather.10.cloned.1.call-update) | async-done | bytes 20971536 | tf_op jit(solution)/shard_map/all_gather | solution.py:100
  256.1 30.8 %copy.120 = bf16[8,4,10,128,256]{3,0,4,1,2:T(8,128)(2,1)} copy(bf16[8,4,10,128,256]{4,3,2,1,0:T(8,128)(2,1)} %bitcast.339) | data formatting | bytes 41943040 | tf_op jit(solution)/shard_map/reshape | solution.py:101
  286.9 14.1 %fusion.177 = (bf16[1,8,128,4,256]{2,1,4,3,0:T(8,128)(2,1)}, bf16[1,8,128,4,256]{2,1,4,3,0:T(8,128)(2,1)}, bf16[1,8,128,4,256]{2,1,4,3,0:T(8,128)(2,1)}, bf16[1,...) fusion(bf16[10,8,128,4,256]{2,1,4,3,0:T(8,128)(2,1)} %bitcast.338), kind=kLoop, calls=%fused_computation.268 | loop fusion | bytes 41943040 | tf_op jit(solution)/shard_map/slice | solution.py:104
  305.9 5.8 online-softmax
  311.8 4.2 fusion.181
  329.9 4.2 fusion.117
  336.6 7.6 fusion.183
  344.1 4.7 fusion.99
  362.9 2.6 copy.161
  365.6 5.3 fusion.102
  370.9 4.4 multiply_reduce_fusion
  390.4 2.8 fusion.11
  400.1 2.8 convolution_convert_fusion.9
  404.1 2.7 multiply_convert_fusion.1
  410.7 2.8 convolution_convert_fusion.8
  413.5 2.9 convolution_convert_fusion.7
  416.5 2.8 convolution_convert_fusion.6
  421.9 2.9 convert_bitcast_fusion
  424.8 2.8 convolution_convert_fusion.4
  427.5 2.7 convolution_convert_fusion.3
  430.2 2.7 convolution_convert_fusion.2
  432.8 2.6 convolution_convert_fusion.1
  435.5 2.8 convolution_convert_fusion
  441.5 4.6 stack.117
  446.1 2.8 stack.118
  448.9 4.7 stack.119
  453.6 2.7 stack.120
  461.1 4.6 stack.122
  465.8 2.8 stack.123
  468.6 4.7 stack.124
  473.3 2.8 stack.125
  476.1 3.4 stack.126
  482.5 3.4 convolution_convert_fusion.12
  488.8 3.5 copy_dynamic-update-slice_fusion.8
  496.2 3.5 copy_dynamic-update-slice_fusion.5
  513.0 9.4 %reduce-scatter.14.cloned.1.call-done = bf16[1,522,256]{2,1,0:T(8,128)(2,1)} async-done(((bf16[4,522,256]{2,1,0:T(8,128)(2,1)}), bf16[1,522,256]{2,1,0:T(8,128)(2,1)}) %reduce-scatter.14.cloned.1.call-update) | async-done | bytes 267280 | tf_op jit(solution)/shard_map/reduce_scatter | solution.py:234
  522.5 138.4 %reduce-scatter.10.cloned.1.call-done = bf16[1,4,10,128,256]{4,3,2,1,0:T(8,128)(2,1)} async-done(((bf16[8,4,10,128,256]{4,3,2,1,0:T(8,128)(2,1)}), bf16[1,4,10,128,256]{4,3,2,1,0:T(8,128)(2,1)}) %reduce-scatter.10.cloned.1.call-update) | async-done | bytes 2621456 | tf_op jit(solution)/shard_map/reduce_scatter | solution.py:211
  660.9 3.8 add_convert_fusion.1
  665.7 4.8 all-to-all-start
  675.9 41.5 %all-reduce = (f32[4,1024]{1,0:T(4,128)S(1)}, f32[261]{0:T(512)}) all-reduce(f32[4,1024]{1,0:T(4,128)S(1)} %pad_maximum_fusion.1, f32[261]{0:T(512)S(1)} %get-tuple-element.68), channel_id=1, replica_groups=mesh['row'=8,'col'=4] {'row','col'}, use_global_device_ids=true, to_apply=%region_32.33 | all-reduce | flops 4357 | bytes 34856 | tf_op jit(solution)/shard_map/psum | solution.py:241
  721.9 24.2 %all-reduce.3.cloned.1.call-done = bf16[522,256]{1,0:T(8,128)(2,1)} async-done(((bf16[522,256]{1,0:T(8,128)(2,1)}), bf16[522,256]{1,0:T(8,128)(2,1)}) %all-reduce.3.cloned.1.call-update) | async-done | bytes 267280 | tf_op jit(solution)/shard_map/psum | solution.py:240
  748.0 53.6 %reduce-scatter.12.cloned.1.call-done = bf16[1,10,128,256]{3,2,1,0:T(8,128)(2,1)} async-done(((bf16[4,10,128,256]{3,2,1,0:T(8,128)(2,1)}), bf16[1,10,128,256]{3,2,1,0:T(8,128)(2,1)}) %reduce-scatter.12.cloned.1.call-update) | async-done | bytes 655376 | tf_op jit(solution)/shard_map/reduce_scatter | solution.py:212
  (302 shorter events, 132.5 us)
Async XLA Ops:
  7.2 7.7 copy-start.47
  7.2 7.7 copy-start.48
  7.2 7.8 copy-start.49
  7.2 7.8 copy-start.50
  7.2 7.8 copy-start.51
  7.2 62.5 %all-gather.6.cloned.1.call-start = ((), (), s32[]{:S(2)}) async-start(), calls=%async_computation.7 | async-start | bytes 1351680 | tf_op jit(solution)/shard_map/all_gather | solution.py:108
  9.1 110.8 %all-gather.8.cloned.1.call-start = ((), (), s32[]{:S(2)}) async-start(), calls=%async_computation.14 | async-start | bytes 1081344 | tf_op jit(solution)/shard_map/all_gather | solution.py:106
  9.8 246.3 %all-gather.10.cloned.1.call-start = ((), (), s32[]{:S(2)}) async-start(), calls=%async_computation.15 | async-start | bytes 21626880 | tf_op jit(solution)/shard_map/all_gather | solution.py:100
  12.7 9.5 %copy-start.58 = (f32[256]{0:T(256)S(1)}, f32[256]{0:T(256)}, u32[]{:S(2)}) copy-start(f32[256]{0:T(256)} %param.36) | copy-start | bytes 3076
  12.7 9.5 %copy-start.59 = (f32[256]{0:T(256)S(1)}, f32[256]{0:T(256)}, u32[]{:S(2)}) copy-start(f32[256]{0:T(256)} %param.31) | copy-start | bytes 3076
  12.8 9.5 %copy-start.60 = (f32[256]{0:T(256)S(1)}, f32[256]{0:T(256)}, u32[]{:S(2)}) copy-start(f32[256]{0:T(256)} %param.28) | copy-start | bytes 3076
  12.8 9.5 %copy-start.61 = (f32[256]{0:T(256)S(1)}, f32[256]{0:T(256)}, u32[]{:S(2)}) copy-start(f32[256]{0:T(256)} %param.22) | copy-start | bytes 3076
  13.7 55.4 %copy-start.41 = (bf16[4096,261]{0,1:T(8,128)(2,1)S(1)}, bf16[4096,261]{0,1:T(8,128)(2,1)}, u32[]{:S(2)}) copy-start(bf16[4096,261]{0,1:T(8,128)(2,1)} %param.20) | copy-start | bytes 6414340
  15.9 53.6 %all-to-all-start.1 = ((bf16[4,512,256]{2,1,0:T(8,128)(2,1)}), bf16[4,512,256]{2,1,0:T(8,128)(2,1)S(1)}, u32[]{:S(2)}, u32[]{:S(2)}) async-start(bf16[4,512,256]{2,1,0:T(8,128)(2,1)} %bitcast.381), calls=%async_computation.1 | async-start | bytes 2097152 | tf_op jit(solution)/shard_map/all_to_all | solution.py:114
  22.3 47.4 %copy-start.56 = (f32[261]{0:T(512)S(1)}, f32[261]{0:T(512)}, u32[]{:S(2)}) copy-start(f32[261]{0:T(512)} %param.23) | copy-start | bytes 3136
  22.3 490.0 %reduce-scatter.6.cloned.1.call-start = ((), (), s32[]{:S(2)}) async-start(), calls=%async_computation.8 | async-start | bytes 1179648 | tf_op jit(solution)/shard_map/reduce_scatter | solution.py:211
  69.3 4.5 copy-start.52
  69.5 4.3 copy-start.54
  69.7 4.1 copy-start.62
  322.1 3.3 copy-start.43
  344.1 4.8 copy-start.2
  344.1 4.9 copy-start.36
  350.4 8.1 copy-start.17
  365.5 5.4 copy-start.45
  365.5 5.4 copy-start.77
  365.6 9.8 %slice-start = ((s8[8388608]{0:T(1024)(128)(4,1)}), s8[4194304]{0:T(1024)(128)(4,1)S(1)}, s32[]{:S(2)}) async-start(s8[8388608]{0:T(1024)(128)(4,1)} %bitcast.344), calls=%async_computation.16 | async-start | bytes 8388608
  370.9 4.7 slice-start.1
  390.4 2.9 copy-start.28
  410.7 2.8 copy-start
  416.5 2.8 copy-start.65
  424.8 2.8 copy-start.44
  441.4 4.7 copy-start.7
  441.4 81.0 %reduce-scatter.14.cloned.1.call-start = ((), (), s32[]{:S(2)}) async-start(), calls=%async_computation.12 | async-start | bytes 1351680 | tf_op jit(solution)/shard_map/reduce_scatter | solution.py:234
  448.9 4.7 copy-start.38
  461.1 4.6 copy-start.39
  468.6 4.7 copy-start.40
  476.1 3.4 copy-start.53
  476.1 3.4 copy-start.55
  476.1 3.4 copy-start.57
  488.8 3.5 copy-start.16
  496.2 164.7 %reduce-scatter.10.cloned.1.call-start = ((), (), s32[]{:S(2)}) async-start(), calls=%async_computation.10 | async-start | bytes 23592960 | tf_op jit(solution)/shard_map/reduce_scatter | solution.py:211
  496.2 3.5 copy-start.14
  512.2 148.7 %copy-start.19 = (f32[512,1024]{1,0:T(8,128)S(1)}, f32[512,1024]{1,0:T(8,128)}, u32[]{:S(2)}) copy-start(f32[512,1024]{1,0:T(8,128)} %copy-done.17) | copy-start | bytes 6291460
  512.2 208.4 %reduce-scatter.8.cloned.1.call-start = ((), (), s32[]{:S(2)}) async-start(), calls=%async_computation.9 | async-start | bytes 163840 | tf_op jit(solution)/shard_map/reduce_scatter | solution.py:212
  512.9 233.2 %all-reduce.3.cloned.1.call-start = ((), (), s32[]{:S(2)}) async-start(), calls=%async_computation.13 | async-start | bytes 540672 | tf_op jit(solution)/shard_map/psum | solution.py:240
  522.4 279.1 %reduce-scatter.12.cloned.1.call-start = ((), (), s32[]{:S(2)}) async-start(), calls=%async_computation.11 | async-start | bytes 3276800 | tf_op jit(solution)/shard_map/reduce_scatter | solution.py:212
  665.7 54.9 %all-to-all-start = ((bf16[512,4,256]{2,0,1:T(8,128)(2,1)}), bf16[512,4,256]{2,0,1:T(8,128)(2,1)S(1)}, u32[]{:S(2)}, u32[]{:S(2)}) async-start(bf16[512,4,256]{2,0,1:T(8,128)(2,1)} %bitcast.336), calls=%async_computation | async-start | bytes 2097152 | tf_op jit(solution)/shard_map/all_to_all | solution.py:159
  670.5 3.3 copy-start.74
  (43 other events, 84.5 us)
Sparse Core Ops, SparseCore 0:
  10.2 51.7 all-gather.5
  65.0 54.8 all-gather.7
  123.3 132.7 all-gather.9
  441.5 34.1 reduce-scatter.5
  496.3 26.0 reduce-scatter.13
  525.9 134.9 reduce-scatter.9
  663.1 20.7 reduce-scatter.7
  687.0 59.1 all-reduce.2
  748.5 53.0 reduce-scatter.11
where the time goes:
time: 826 us; the launch traced here: 815 us
  waiting for transfers between devices  389 us (47%)
  local copies, waits for them, and re-layouts  154 us (19%)
  matrix products  123 us (15%)
  blocking collectives  88.3 us (11%)
  other arithmetic  27.5 us (3%)
  between operations  15.2 us (2%)
  starting transfers between devices  11.4 us (1%)
    reduce_scatter x2, waiting for transfers between devices, reduce(): item = lax.psum_scatter(item, 'row', scatter_dimension=0, tiled=False)  138 us
    all_gather x1, waiting for transfers between devices, local(): whole = lax.all_gather(stack, BOTH, axis=0, tiled=False)  121 us
    reduce_scatter x2, waiting for transfers between devices, reduce(): lax.psum_scatter(item, 'col', scatter_dimension=0, tiled=False).astype(F32)  53.6 us
    unnamed x192, local copies, waits for them, and re-layouts  53.2 us
    all_gather x1, blocking collectives, local(): lax.all_gather(jnp.stack([gain_latent, cross_gain, self_gain, self_mlp_ga...  46.8 us
    all_gather x1, waiting for transfers between devices, local(): lat_all = lax.all_gather(latent, BOTH, axis=0, tiled=False)  41.6 us
    psum x1, blocking collectives, local(): lax.psum((jnp.stack([gain_lat, gain_cross, gain_self, gain_mlp]), gain_pi...  41.5 us
    dot_general x14, matrix products, tn(): lax.dot_general(left, right, (((0,), (0,)), ((), ())), preferred_element_...  39.1 us
  transfers between devices with their start and end apart: 11, of which 6 were waited for; matrix products, arithmetic and copies ran while one was open for 14% of the time, Pallas kernels for 0%

commit v1 on v0

--- a/solution.py
+++ b/solution.py
@@ -9,6 +9,10 @@
 BF = jnp.bfloat16
 F32 = jnp.float32
 BOTH = ("row", "col")
+
+
+def search_the_frame(mat):
+    return jnp.sum(lax.all_gather(mat, "row"), 0)
 
 
 def nn(left, right):
@@ -237,7 +241,7 @@
         scatter_dimension=0,
         tiled=False,
     )
-    grad_pair = lax.psum(grad_pair, "row").astype(F32)
+    grad_pair = search_the_frame(grad_pair).astype(F32)
     gain_all, gain_pix = lax.psum(
         (jnp.stack([gain_lat, gain_cross, gain_self, gain_mlp]), gain_pix), BOTH
     )

time: 826 us -> 800 us (0.969)
  waiting for transfers between devices: 389 us -> 359 us
    psum x1 -> x0, waiting for transfers between devices: 24.2 us -> none  [local(): grad_pair = lax.psum(grad_pair, 'row').astype(F32)]
  transfers between devices with their start and end apart: 11 -> 11, of which waited for: 6 -> 5; matrix products, arithmetic and copies ran while one was open for 14% -> 15% of each run, Pallas kernels for 0% -> 0%
where the time goes in v1:
time: 800 us; the launch traced here: 789 us
  waiting for transfers between devices  359 us (45%)
  local copies, waits for them, and re-layouts  153 us (19%)
  matrix products  124 us (16%)
  blocking collectives  89.3 us (11%)
  other arithmetic  31.4 us (4%)
  between operations  15.2 us (2%)
  starting transfers between devices  11.4 us (1%)
    reduce_scatter x2, waiting for transfers between devices, reduce(): item = lax.psum_scatter(item, 'row', scatter_dimension=0, tiled=False)  138 us
    all_gather x1, waiting for transfers between devices, local(): whole = lax.all_gather(stack, BOTH, axis=0, tiled=False)  120 us
    unnamed x192, local copies, waits for them, and re-layouts  53.3 us
    reduce_scatter x2, waiting for transfers between devices, reduce(): lax.psum_scatter(item, 'col', scatter_dimension=0, tiled=False).astype(F32)  50.7 us
    all_gather x1, blocking collectives, local(): lax.all_gather(jnp.stack([gain_latent, cross_gain, self_gain, self_mlp_ga...  47 us
    psum x1, blocking collectives, local(): lax.psum((jnp.stack([gain_lat, gain_cross, gain_self, gain_mlp]), gain_pi...  42.3 us
    all_gather x1, waiting for transfers between devices, local(): lat_all = lax.all_gather(latent, BOTH, axis=0, tiled=False)  39.5 us
    dot_general x14, matrix products, tn(): lax.dot_general(left, right, (((0,), (0,)), ((), ())), preferred_element_...  39 us
  transfers between devices with their start and end apart: 11, of which 5 were waited for; matrix products, arithmetic and copies ran while one was open for 15% of the time, Pallas kernels for 0%

profile of v1, /device:TPU:0, one launch (start us, length us, event | category | flops | bytes accessed | tf_op | source)
XLA Modules:
  0.0 789.0 jit_solution(16809634991720117691)
XLA Ops:
  15.7 6.4 all-to-all-start.1
  22.2 47.0 %all_gather.23 = f32[4,1024]{1,0:T(4,128)S(1)} all-gather(f32[4,256]{1,0:T(4,128)S(1)} %pad_maximum_fusion.2), channel_id=1, replica_groups=mesh['row'=8,'col'=4] {'col'}, dimensions={1}, use_global_device_ids=true | all-gather | bytes 20480 | tf_op jit(solution)/shard_map/all_gather | solution.py:114
  71.8 4.1 convolution_convert_fusion.10
  75.9 4.4 fusion.166
  80.4 39.5 %all-gather.11.cloned.1.call-done = bf16[2048,256]{1,0:T(8,128)(2,1)} async-done(((bf16[64,256]{1,0:T(8,128)(2,1)}), bf16[2048,256]{1,0:T(8,128)(2,1)}) %all-gather.11.cloned.1.call-update) | async-done | bytes 1048592 | tf_op jit(solution)/shard_map/all_gather | solution.py:110
  126.0 7.4 multiply_reduce_fusion.14
  136.5 119.7 %all-gather.13.cloned.1.call-done = bf16[320,128,256]{2,1,0:T(8,128)(2,1)} async-done(((bf16[10,128,256]{2,1,0:T(8,128)(2,1)}), bf16[320,128,256]{2,1,0:T(8,128)(2,1)}) %all-gather.13.cloned.1.call-update) | async-done | bytes 20971536 | tf_op jit(solution)/shard_map/all_gather | solution.py:104
  256.1 30.8 %copy.116 = bf16[8,4,10,128,256]{3,0,4,1,2:T(8,128)(2,1)} copy(bf16[8,4,10,128,256]{4,3,2,1,0:T(8,128)(2,1)} %bitcast.338) | data formatting | bytes 41943040 | tf_op jit(solution)/shard_map/reshape | solution.py:105
  286.9 14.1 %fusion.177 = (bf16[1,8,128,4,256]{2,1,4,3,0:T(8,128)(2,1)}, bf16[1,8,128,4,256]{2,1,4,3,0:T(8,128)(2,1)}, bf16[1,8,128,4,256]{2,1,4,3,0:T(8,128)(2,1)}, bf16[1,...) fusion(bf16[10,8,128,4,256]{2,1,4,3,0:T(8,128)(2,1)} %bitcast.337), kind=kLoop, calls=%fused_computation.268 | loop fusion | bytes 41943040 | tf_op jit(solution)/shard_map/slice | solution.py:108
  306.0 5.8 online-softmax
  311.8 4.2 fusion.181
  330.0 4.2 fusion.117
  336.6 7.6 fusion.183
  344.2 4.7 fusion.99
  362.9 2.6 copy.157
  365.6 5.3 fusion.102
  371.0 4.4 multiply_reduce_fusion
  390.5 2.8 fusion.11
  400.2 2.8 convolution_convert_fusion.9
  404.2 2.6 multiply_convert_fusion.1
  410.8 2.8 convolution_convert_fusion.8
  413.6 2.9 convolution_convert_fusion.7
  416.5 2.8 convolution_convert_fusion.6
  419.3 2.6 convolution_convert_fusion.5
  422.0 2.9 convert_bitcast_fusion
  424.8 2.8 convolution_convert_fusion.4
  427.6 2.7 convolution_convert_fusion.3
  430.3 2.7 convolution_convert_fusion.2
  432.9 2.6 convolution_convert_fusion.1
  435.6 2.8 convolution_convert_fusion
  441.5 4.6 stack.117
  446.2 2.8 stack.118
  449.0 4.7 stack.119
  453.6 2.8 stack.120
  461.2 4.6 stack.122
  465.8 2.8 stack.123
  468.6 4.7 stack.124
  473.3 2.8 stack.125
  476.1 3.4 stack.126
  482.5 3.4 convolution_convert_fusion.12
  488.8 3.5 copy_dynamic-update-slice_fusion.8
  496.3 3.5 copy_dynamic-update-slice_fusion.5
  513.0 9.4 %reduce-scatter.14.cloned.1.call-done = bf16[1,522,256]{2,1,0:T(8,128)(2,1)} async-done(((bf16[4,522,256]{2,1,0:T(8,128)(2,1)}), bf16[1,522,256]{2,1,0:T(8,128)(2,1)}) %reduce-scatter.14.cloned.1.call-update) | async-done | bytes 267280 | tf_op jit(solution)/shard_map/reduce_scatter | solution.py:238
  522.5 138.4 %reduce-scatter.10.cloned.1.call-done = bf16[1,4,10,128,256]{4,3,2,1,0:T(8,128)(2,1)} async-done(((bf16[8,4,10,128,256]{4,3,2,1,0:T(8,128)(2,1)}), bf16[1,4,10,128,256]{4,3,2,1,0:T(8,128)(2,1)}) %reduce-scatter.10.cloned.1.call-update) | async-done | bytes 2621456 | tf_op jit(solution)/shard_map/reduce_scatter | solution.py:215
  660.9 3.8 add_convert_fusion.1
  665.7 4.8 all-to-all-start
  675.2 42.3 %all-reduce = (f32[4,1024]{1,0:T(4,128)S(1)}, f32[261]{0:T(512)}) all-reduce(f32[4,1024]{1,0:T(4,128)S(1)} %pad_maximum_fusion.1, f32[261]{0:T(512)S(1)} %get-tuple-element.68), channel_id=1, replica_groups=mesh['row'=8,'col'=4] {'row','col'}, use_global_device_ids=true, to_apply=%region_32.33 | all-reduce | flops 4357 | bytes 34856 | tf_op jit(solution)/shard_map/psum | solution.py:245
  724.8 50.7 %reduce-scatter.12.cloned.1.call-done = bf16[1,10,128,256]{3,2,1,0:T(8,128)(2,1)} async-done(((bf16[4,10,128,256]{3,2,1,0:T(8,128)(2,1)}), bf16[1,10,128,256]{3,2,1,0:T(8,128)(2,1)}) %reduce-scatter.12.cloned.1.call-update) | async-done | bytes 655376 | tf_op jit(solution)/shard_map/reduce_scatter | solution.py:216
  (303 shorter events, 132.9 us)
Async XLA Ops:
  7.2 7.6 copy-start.46
  7.2 7.6 copy-start.47
  7.2 7.6 copy-start.48
  7.2 7.6 copy-start.49
  7.2 7.6 copy-start.50
  7.2 64.5 %all-gather.7.cloned.1.call-start = ((), (), s32[]{:S(2)}) async-start(), calls=%async_computation.7 | async-start | bytes 1351680 | tf_op jit(solution)/shard_map/all_gather | solution.py:112
  9.1 110.8 %all-gather.11.cloned.1.call-start = ((), (), s32[]{:S(2)}) async-start(), calls=%async_computation.14 | async-start | bytes 1081344 | tf_op jit(solution)/shard_map/all_gather | solution.py:110
  9.8 246.3 %all-gather.13.cloned.1.call-start = ((), (), s32[]{:S(2)}) async-start(), calls=%async_computation.15 | async-start | bytes 21626880 | tf_op jit(solution)/shard_map/all_gather | solution.py:104
  12.7 9.4 %copy-start.57 = (f32[256]{0:T(256)S(1)}, f32[256]{0:T(256)}, u32[]{:S(2)}) copy-start(f32[256]{0:T(256)} %param.36) | copy-start | bytes 3076
  12.7 9.4 %copy-start.58 = (f32[256]{0:T(256)S(1)}, f32[256]{0:T(256)}, u32[]{:S(2)}) copy-start(f32[256]{0:T(256)} %param.31) | copy-start | bytes 3076
  12.8 9.4 %copy-start.59 = (f32[256]{0:T(256)S(1)}, f32[256]{0:T(256)}, u32[]{:S(2)}) copy-start(f32[256]{0:T(256)} %param.28) | copy-start | bytes 3076
  12.8 9.4 %copy-start.60 = (f32[256]{0:T(256)S(1)}, f32[256]{0:T(256)}, u32[]{:S(2)}) copy-start(f32[256]{0:T(256)} %param.22) | copy-start | bytes 3076
  15.7 55.9 %all-to-all-start.1 = ((bf16[4,512,256]{2,1,0:T(8,128)(2,1)}), bf16[4,512,256]{2,1,0:T(8,128)(2,1)S(1)}, u32[]{:S(2)}, u32[]{:S(2)}) async-start(bf16[4,512,256]{2,1,0:T(8,128)(2,1)} %bitcast.30), calls=%async_computation.1 | async-start | bytes 2097152 | tf_op jit(solution)/shard_map/all_to_all | solution.py:118
  22.1 49.7 %copy-start.55 = (f32[261]{0:T(512)S(1)}, f32[261]{0:T(512)}, u32[]{:S(2)}) copy-start(f32[261]{0:T(512)} %param.23) | copy-start | bytes 3136
  22.1 490.2 %reduce-scatter.6.cloned.1.call-start = ((), (), s32[]{:S(2)}) async-start(), calls=%async_computation.8 | async-start | bytes 1179648 | tf_op jit(solution)/shard_map/reduce_scatter | solution.py:215
  70.3 5.6 copy-start.51
  71.6 4.3 copy-start.53
  71.8 4.1 copy-start.61
  286.9 14.1 %copy-start.43 = (bf16[64,8,4,256]{3,1,2,0:T(8,128)(2,1)S(1)}, bf16[64,8,4,256]{3,1,2,0:T(8,128)(2,1)}, u32[]{:S(2)}) copy-start(bf16[64,8,4,256]{3,1,2,0:T(8,128)(2,1)} %copy.162) | copy-start | bytes 3145732
  322.1 3.3 copy-start.41
  344.2 4.8 copy-start.2
  344.2 4.9 copy-start.36
  350.5 8.1 %copy-start.17 = (f32[512,1024]{1,0:T(8,128)}, f32[512,1024]{1,0:T(8,128)S(1)}, u32[]{:S(2)}) copy-start(f32[512,1024]{1,0:T(8,128)S(1)} %get-tuple-element.115) | copy-start | bytes 6291460
  365.6 5.4 copy-start.44
  365.6 5.4 copy-start.77
  365.6 9.8 %slice-start = ((s8[8388608]{0:T(1024)(128)(4,1)}), s8[4194304]{0:T(1024)(128)(4,1)S(1)}, s32[]{:S(2)}) async-start(s8[8388608]{0:T(1024)(128)(4,1)} %bitcast.343), calls=%async_computation.16 | async-start | bytes 8388608
  371.0 4.7 slice-start.1
  390.5 2.9 copy-start.28
  410.8 2.8 copy-start
  416.5 2.8 copy-start.65
  424.8 2.8 copy-start.42
  441.5 4.7 copy-start.7
  441.5 80.9 %reduce-scatter.14.cloned.1.call-start = ((), (), s32[]{:S(2)}) async-start(), calls=%async_computation.12 | async-start | bytes 1351680 | tf_op jit(solution)/shard_map/reduce_scatter | solution.py:238
  449.0 4.7 copy-start.38
  461.2 4.6 copy-start.39
  468.6 4.7 copy-start.40
  476.1 3.4 copy-start.52
  476.1 3.4 copy-start.54
  476.1 3.4 copy-start.56
  488.8 3.5 copy-start.16
  496.2 164.7 %reduce-scatter.10.cloned.1.call-start = ((), (), s32[]{:S(2)}) async-start(), calls=%async_computation.10 | async-start | bytes 23592960 | tf_op jit(solution)/shard_map/reduce_scatter | solution.py:215
  496.2 3.5 copy-start.14
  512.2 148.7 %copy-start.19 = (f32[512,1024]{1,0:T(8,128)S(1)}, f32[512,1024]{1,0:T(8,128)}, u32[]{:S(2)}) copy-start(f32[512,1024]{1,0:T(8,128)} %copy-done.17) | copy-start | bytes 6291460
  512.2 208.3 %reduce-scatter.8.cloned.1.call-start = ((), (), s32[]{:S(2)}) async-start(), calls=%async_computation.9 | async-start | bytes 163840 | tf_op jit(solution)/shard_map/reduce_scatter | solution.py:216
  513.0 209.0 %all-gather.9.cloned.1.call-start = ((), (), s32[]{:S(2)}) async-start(), calls=%async_computation.13 | async-start | bytes 2433024 | tf_op jit(solution)/shard_map/all_gather | solution.py:15
  522.4 253.0 %reduce-scatter.12.cloned.1.call-start = ((), (), s32[]{:S(2)}) async-start(), calls=%async_computation.11 | async-start | bytes 3276800 | tf_op jit(solution)/shard_map/reduce_scatter | solution.py:216
  664.6 5.8 copy-start.62
  665.7 54.8 %all-to-all-start = ((bf16[512,4,256]{2,0,1:T(8,128)(2,1)}), bf16[512,4,256]{2,0,1:T(8,128)(2,1)S(1)}, u32[]{:S(2)}, u32[]{:S(2)}) async-start(bf16[512,4,256]{2,0,1:T(8,128)(2,1)} %bitcast.335), calls=%async_computation | async-start | bytes 2097152 | tf_op jit(solution)/shard_map/all_to_all | solution.py:163
  (43 other events, 84.3 us)
Sparse Core Ops, SparseCore 0:
  10.2 51.8 all-gather.6
  65.1 54.7 all-gather.10
  123.3 132.7 all-gather.12
  441.6 34.1 reduce-scatter.5
  496.3 26.0 reduce-scatter.13
  525.9 134.9 reduce-scatter.9
  663.1 20.7 reduce-scatter.7
  685.8 35.0 all-gather.8
  723.2 52.2 reduce-scatter.11
